TPU v7x, 32 devices: a whole 2x2x4 slice. The times are simulated.
32 devices in a mesh: orb: 4 (over z), box: 8 (over y, x, core).
Axes of the slice: x: 2, y: 2, z: 4, core: 2. Of those that a mesh axis runs over, the one named last changes fastest.
Arguments:
- coarse: bfloat16 [4, 8, 729, 1024], P('orb', None, None, 'box'), may hold values from -1.5 to 1.5
- wavelets: bfloat16 [4, 7, 729, 1024], P('orb', None, None, 'box'), may hold values from -1.5 to 1.5
- leaf_flags: int32 [4, 1024], P('orb', 'box'), may hold values 0 or 1
- child_key1: int32 [1024], P('box'), may hold values from 0 to 8191, as said below
- child_key2: int32 [2048], P('box'), may hold values from 0 to 8191, as said below
- counts: int32 [8], P('box'), may hold values from 128 to 256, as said below
Outputs:
- density: float32 [729, 2048], P(None, 'box')
Inputs may be any that keep to these rules, and one draw needn't show every extreme that they name: `child_key1`: within each curve range of 128 entries the keys rise and name distinct children; each parent lies in the same range or among the last 32 boxes of the range before; every range but the first has an entry naming a child of the first of those 32 boxes. `child_key2`: within each curve range of 256 entries the keys rise and name distinct children; each parent lies in the same range or among the last 32 boxes of the range before; every range but the first has an entry naming a child of the first of those 32 boxes. `counts`: some range is full in every draw and some range holds the fewest.
All inputs are finite; a program needn't handle non-finite values. No bound on the sum of `leaf_flags` on one device may be relied on, other than what follows from the above.
Results may differ from a plain program's by a relative error of at most 0.0003.
Values may be sent and summed in bfloat16 or wider, within the bound.
A program may use at most 64 MiB of HBM per device.

v0:
```python
import math

import jax
import jax.numpy as jnp
import numpy as np
from jax import lax
from jax.experimental import pallas as pl
from jax.experimental.pallas import tpu as pltpu
from jax.sharding import PartitionSpec as P

SPILL = 32


def shifted_2(value, axis, steps):
    count = lax.axis_size(axis)
    first, last = (max(0, -steps), min(count, count - steps))
    return lax.ppermute(value, axis, [(source, source + steps) for source in range(first, last)])


def legendre_pair(order, where):
    before = where * 0.0 + 1.0
    value = where
    for degree in range(1, order):
        before, value = (value, ((2 * degree + 1) * where * value - degree * before) / (degree + 1))
    return (value, before)


def gauss_rule(order):
    nodes = np.cos(np.pi * (np.arange(order) + 0.75) / (order + 0.5))
    for repeat in range(40):
        value, before = legendre_pair(order, nodes)
        slope = order * (nodes * value - before) / (nodes * nodes - 1.0)
        nodes = nodes - value / slope
    value, before = legendre_pair(order, nodes)
    slope = order * (nodes * value - before) / (nodes * nodes - 1.0)
    weights = 2.0 / ((1.0 - nodes * nodes) * slope * slope)
    return (nodes[::-1], weights[::-1])


def legendre_basis(where):
    shifted = 2.0 * where - 1.0
    rows = [shifted * 0.0 + 1.0, shifted]
    for degree in range(1, 8):
        rows.append(
            ((2 * degree + 1) * shifted * rows[degree] - degree * rows[degree - 1]) / (degree + 1)
        )
    scale = np.sqrt(2.0 * np.arange(9) + 1.0)[:, None]
    return np.stack(rows, 0) * scale


def complement_rows(scaling_rows):
    members = [scaling_rows[index] for index in range(9)]
    kept = []
    identity = np.eye(18)
    for column in range(18):
        vector = identity[column]
        for passes in range(2):
            for member in members + kept:
                vector = vector - np.dot(member, vector) * member
        length = np.sqrt(np.dot(vector, vector))
        if length > 0.1 and len(kept) < 9:
            kept.append(vector / length)
    return np.stack(kept, 0)


def wavelet_tables():
    nodes, weights = gauss_rule(24)
    points = 0.5 * (nodes + 1.0)
    halves = 0.5 * weights
    lower = legendre_basis(0.5 * points) * halves @ legendre_basis(points).T / math.sqrt(2.0)
    upper = legendre_basis(0.5 * points + 0.5) * halves @ legendre_basis(points).T / math.sqrt(2.0)
    scaling_rows = np.concatenate([lower, upper], 1)
    wavelet_rows = complement_rows(scaling_rows)
    matrix = np.concatenate([scaling_rows, wavelet_rows], 0).reshape(2, 9, 2, 9)
    gauss, gauss_weights = gauss_rule(9)
    quad = legendre_basis(0.5 * (gauss + 1.0)).T * np.sqrt(0.5 * gauss_weights)[:, None]
    return (matrix.reshape(18, 2, 9), quad)


ROWS = 729
PADDED = 800
GROUPS = ((0, 1), (2, 3), (4, 5), (6, 7), (8, 9, 10))
QUARTER = 192


def local_keys(key_ref, boxes):
    key = key_ref[...] - lax.axis_index("box") * (8 * boxes)
    return (lax.shift_right_arithmetic(key, 3), key & 7)


def spread_matrix(boxes, group):
    source = lax.broadcasted_iota(jnp.int32, (boxes, 128), 0)
    target = lax.broadcasted_iota(jnp.int32, (boxes, 128), 1)
    hit = (source - (boxes - SPILL) == target - SPILL * group) & (source >= boxes - SPILL)
    return hit.astype(jnp.float32).astype(jnp.bfloat16)


def pick_own(column, boxes):
    row = lax.broadcasted_iota(jnp.int32, (boxes, column.shape[1]), 0)
    return (row == column).astype(jnp.float32)


def pick_spilled(column, group):
    row = lax.broadcasted_iota(jnp.int32, (128, column.shape[1]), 0)
    hit = (row == column + SPILL * (group + 1)) & (column < 0)
    return hit.astype(jnp.float32)


def fill_coefficients(coef_ref, octant, table):
    for axis in range(3):
        bit = jnp.broadcast_to((octant >> axis) & 1, (8, 128)) == 1
        for k in range(18):
            for f in range(9):
                coef_ref[axis * 162 + k * 9 + f] = jnp.where(
                    bit, np.float32(table[k, 1, f]), np.float32(table[k, 0, f])
                )


def contract(source_ref, low, high, coef_ref, axis, store):
    for group in GROUPS:
        inputs = [
            [
                source_ref[block, pl.ds(l + 72 * t, 8, stride=9), :]
                for block in (low, high)
                for l in range(9)
            ]
            for t in group
        ]
        for f in range(9):
            sums = [None] * len(group)
            for k in range(18):
                weight = coef_ref[axis * 162 + k * 9 + f]
                for n in range(len(group)):
                    term = weight * inputs[n][k]
                    sums[n] = term if sums[n] is None else sums[n] + term
            for n, t in enumerate(group):
                store(81 * f + 8 * t, min(8, 81 - 8 * t), sums[n])


def transform(x_ref, a_ref, b_ref, coef_ref, finish):
    def first(index, carry):
        def store(row, count, value):
            a_ref[index, row : row + count, :] = value[:count]

        contract(x_ref, 2 * index, 2 * index + 1, coef_ref, 0, store)
        return carry

    lax.fori_loop(0, 4, first, 0)

    def second(index, carry):
        def store(row, count, value):
            b_ref[index, row : row + count, :] = value[:count]

        contract(a_ref, 2 * index, 2 * index + 1, coef_ref, 1, store)
        return carry

    lax.fori_loop(0, 2, second, 0)
    contract(b_ref, 0, 1, coef_ref, 2, finish)


def dot(left, right):
    return jnp.dot(left, right, preferred_element_type=jnp.float32)


def pack_coarse_kernel(coarse_ref, out_ref):
    boxes = coarse_ref.shape[-1]
    spread = [spread_matrix(boxes, g) for g in range(4)]
    for h in range(2):
        total = dot(coarse_ref[h], spread[0])
        for g in range(1, 4):
            total = total + dot(coarse_ref[2 * g + h], spread[g])
        out_ref[h] = total.astype(jnp.bfloat16)


def pack_waves_kernel(waves_ref, flags_ref, out_ref):
    boxes = waves_ref.shape[-1]
    keep = (1 - flags_ref[...]).astype(jnp.float32)
    source = lax.broadcasted_iota(jnp.int32, (128, SPILL), 0)
    spread = [spread_matrix(boxes, g) for g in range(4)]
    packed_keep = sum(dot(jnp.broadcast_to(keep, (16, boxes)).astype(jnp.bfloat16), s) for s in spread)
    packed_keep = packed_keep[:1]
    for h in range(2):
        total = jnp.zeros((ROWS, 128), jnp.float32)
        for g in range(4):
            if 2 * g + h > 0:
                total = total + dot(waves_ref[2 * g + h - 1], spread[g])
        out_ref[h] = (total * packed_keep).astype(jnp.bfloat16)


def first_kernel(coarse_ref, halo_ref, key_ref, s_ref, spill_ref, x_ref, a_ref, b_ref, coef_ref, fine_ref, *, table):
    boxes = coarse_ref.shape[-1]
    column, octant = local_keys(key_ref, boxes)
    fill_coefficients(coef_ref, octant, table)
    own = pick_own(column, boxes)
    for g in range(4):
        pick = jnp.concatenate([own, pick_spilled(column, g)], 0).astype(jnp.bfloat16)
        for h in range(2):
            both = jnp.concatenate([coarse_ref[2 * g + h], halo_ref[h]], 1)
            x_ref[2 * g + h, 0:ROWS, :] = dot(both, pick)
    fine_ref[ROWS - 1 : 4 * QUARTER, :] = jnp.zeros((4 * QUARTER - ROWS + 1, 128), jnp.float32)

    def store(row, count, value):
        fine_ref[row : row + count, :] = value[:count]

    transform(x_ref, a_ref, b_ref, coef_ref, store)
    fine = fine_ref[...]
    high = fine.astype(jnp.bfloat16)
    low = (fine - high.astype(jnp.float32)).astype(jnp.bfloat16)
    s_ref[0] = high
    s_ref[1] = low
    for part, whole in enumerate((high, low)):
        total = None
        for g in range(4):
            term = dot(whole[QUARTER * g : QUARTER * (g + 1)], spread_matrix(boxes, g))
            total = term if total is None else total + term
        spill_ref[part] = total.astype(jnp.bfloat16)


def second_kernel(
    counts_ref, waves_ref, halo_ref, flags_ref, s_ref, spill_ref, key_ref, out_ref, x_ref, a_ref, b_ref, coef_ref, *, table
):
    boxes = waves_ref.shape[-1]
    column, octant = local_keys(key_ref, boxes)
    fill_coefficients(coef_ref, octant, table)
    own = pick_own(column, boxes)
    keep = (1 - flags_ref[...]).astype(jnp.float32)
    kept = dot(jnp.broadcast_to(keep, (16, boxes)).astype(jnp.bfloat16), own.astype(jnp.bfloat16))
    own_kept = own * kept[:1]
    for g in range(4):
        spilled = pick_spilled(column, g)
        pick = jnp.concatenate([own, spilled], 0).astype(jnp.bfloat16)
        total = None
        for part in range(2):
            both = jnp.concatenate([s_ref[part, QUARTER * g : QUARTER * (g + 1), :], spill_ref[part]], 1)
            term = dot(both, pick)
            total = term if total is None else total + term
        x_ref[0, QUARTER * g : QUARTER * (g + 1), :] = total
        pick = jnp.concatenate([own_kept, spilled], 0).astype(jnp.bfloat16)
        for h in range(2):
            if 2 * g + h > 0:
                both = jnp.concatenate([waves_ref[2 * g + h - 1], halo_ref[h]], 1)
                x_ref[2 * g + h, 0:ROWS, :] = dot(both, pick)
    slot = pl.program_id(0) * 128 + lax.broadcasted_iota(jnp.int32, (8, 128), 1)
    live = jnp.where(slot < counts_ref[0], 2.0, 0.0).astype(jnp.float32)

    def store(row, count, value):
        out_ref[row : row + count, :] = (value * value * live)[:count]

    transform(x_ref, a_ref, b_ref, coef_ref, store)


def transform_scratch():
    return [
        pltpu.VMEM((8, PADDED, 128), jnp.float32),
        pltpu.VMEM((4, PADDED, 128), jnp.float32),
        pltpu.VMEM((2, PADDED, 128), jnp.float32),
        pltpu.VMEM((3 * 162, 8, 128), jnp.float32),
    ]


def shards(coarse, wavelets, leaf_flags, child_key1, child_key2, counts):
    matrix, quad = wavelet_tables()
    valued = np.einsum("kop,gp->kog", matrix, quad)
    boxes = coarse.shape[-1]
    slots = child_key2.shape[0]
    vmem = pl.BlockSpec(memory_space=pltpu.VMEM)
    packed = jax.ShapeDtypeStruct((2, ROWS, 128), jnp.bfloat16)
    coarse, wavelets = coarse[0], wavelets[0]
    params = pltpu.CompilerParams(vmem_limit_bytes=48 * 1024 * 1024)
    coarse_halo = pl.pallas_call(
        pack_coarse_kernel, out_shape=packed, in_specs=[vmem], out_specs=vmem, compiler_params=params
    )(coarse)
    coarse_halo = shifted_2(coarse_halo, "box", 1)
    waves_halo = pl.pallas_call(
        pack_waves_kernel, out_shape=packed, in_specs=[vmem] * 2, out_specs=vmem, compiler_params=params
    )(wavelets, leaf_flags)
    waves_halo = shifted_2(waves_halo, "box", 1)
    scaling, spill = pl.pallas_call(
        lambda *refs: first_kernel(*refs, table=matrix),
        out_shape=(
            jax.ShapeDtypeStruct((2, 4 * QUARTER, 128), jnp.bfloat16),
            jax.ShapeDtypeStruct((2, QUARTER, 128), jnp.bfloat16),
        ),
        in_specs=[vmem] * 3,
        out_specs=(vmem, vmem),
        scratch_shapes=transform_scratch() + [pltpu.VMEM((4 * QUARTER, 128), jnp.float32)],
        compiler_params=params,
    )(coarse, coarse_halo, child_key1.reshape(1, boxes))
    spill = shifted_2(spill, "box", 1)

    def whole(shape):
        return pl.BlockSpec(shape, lambda step: (0,) * len(shape))

    partial_density = pl.pallas_call(
        lambda *refs: second_kernel(*refs, table=valued),
        grid=(slots // 128,),
        out_shape=jax.ShapeDtypeStruct((ROWS, slots), jnp.float32),
        in_specs=[
            pl.BlockSpec(memory_space=pltpu.SMEM),
            whole(wavelets.shape),
            whole(packed.shape),
            whole(leaf_flags.shape),
            whole(scaling.shape),
            whole(spill.shape),
            pl.BlockSpec((1, 128), lambda step: (0, step)),
        ],
        out_specs=pl.BlockSpec((ROWS, 128), lambda step: (0, step)),
        scratch_shapes=transform_scratch(),
        compiler_params=params,
    )(counts, wavelets, waves_halo, leaf_flags, scaling, spill, child_key2.reshape(1, slots))
    return lax.psum(partial_density, "orb")


def solution(mesh):
    in_specs = (
        P("orb", None, None, "box"),
        P("orb", None, None, "box"),
        P("orb", "box"),
        P("box"),
        P("box"),
        P("box"),
    )
    out_specs = P(None, "box")
    return jax.shard_map(shards, mesh=mesh, in_specs=in_specs, out_specs=out_specs, check_vma=False)
```

profile of v0, /device:TPU:0, one launch (start us, length us, event | category | flops | bytes accessed | tf_op | source)
XLA Modules:
  0.0 94.0 jit_solution(10202658744628907129)
XLA Ops:
  6.5 0.0 all-reduce.2.cloned.1.call-start
  6.5 1.6 %copy.9 = bf16[1,8,729,128]{3,2,1,0:T(8,128)(2,1)S(1)} copy(bf16[1,8,729,128]{3,1,2,0:T(8,128)(2,1)} %param.6) | data formatting | bytes 2985984 | tf_op args[0]
  8.1 0.0 copy-start
  8.1 0.0 copy-start.1
  8.1 0.0 copy-start.3
  8.2 0.5 shard_map.65
  8.7 2.4 %collective-permute-start.1 = (bf16[2,729,128]{2,1,0:T(8,128)(2,1)S(1)}, bf16[2,729,128]{2,1,0:T(8,128)(2,1)S(1)}, u32[]{:S(2)}, u32[]{:S(2)}) collective-permute-start(bf16[2,729,128]{2,1,0:T(8,128)(2,1)S(1)} %shard_map.65), channel_id=1, source_target_pairs={{0,1},{1,2},{2,3},{3,4},{4,5},{5,6},{6,7},{8,9},{9,10},{10,11},{11... | collective-permute-start | bytes 1119752 | tf_op jit(solution)/shard_map/ppermute | solution.py:17
  11.1 0.0 copy-done
  11.1 0.0 copy-done.1
  11.1 0.0 copy-start.2
  11.1 0.5 shard_map.64
  11.7 4.5 %collective-permute-start = (bf16[2,729,128]{2,1,0:T(8,128)(2,1)S(1)}, bf16[2,729,128]{2,1,0:T(8,128)(2,1)S(1)}, u32[]{:S(2)}, u32[]{:S(2)}) collective-permute-start(bf16[2,729,128]{2,1,0:T(8,128)(2,1)S(1)} %shard_map.64), channel_id=1, source_target_pairs={{0,1},{1,2},{2,3},{3,4},{4,5},{5,6},{6,7},{8,9},{9,10},{10,11},{11... | collective-permute-start | bytes 1119752 | tf_op jit(solution)/shard_map/ppermute | solution.py:17
  16.2 0.0 collective-permute-done.1.refs_1_
  16.2 0.0 copy-done.3
  16.2 4.8 %shard_map.66 = (bf16[2,768,128]{2,1,0:T(8,128)(2,1)S(1)}, bf16[2,192,128]{2,1,0:T(8,128)(2,1)S(1)}) custom-call(bf16[8,729,128]{2,1,0:T(8,128)(2,1)S(1)} %bitcast.7, bf16[2,729,128]{2,1,0:T(8,128)(2,1)S(1)} %collective-permute-done.1.refs_1_, s32[1,128]{1,0:T(1,128)S(1)} %bitcast.11), custom_call_target="tpu_custom_call" | custom-call | tf_op jit(solution)/shard_map/pallas_call | solution.py:278
  21.0 3.9 %collective-permute-start.2 = (bf16[2,192,128]{2,1,0:T(8,128)(2,1)S(1)}, bf16[2,192,128]{2,1,0:T(8,128)(2,1)S(1)}, u32[]{:S(2)}, u32[]{:S(2)}) collective-permute-start(bf16[2,192,128]{2,1,0:T(8,128)(2,1)S(1)} %get-tuple-element.8), channel_id=1, source_target_pairs={{0,1},{1,2},{2,3},{3,4},{4,5},{5,6},{6,7},{8,9},{9,10},{10,11},{11... | collective-permute-start | bytes 294920 | tf_op jit(solution)/shard_map/ppermute | solution.py:17
  25.6 0.0 collective-permute-done.refs_2_
  25.6 0.3 collective-permute-done.2.refs_5_
  25.8 0.0 copy-done.2
  25.8 10.2 %shard_map.67 = f32[729,256]{1,0:T(8,128)} custom-call(s32[1]{0:T(128)S(6)} %copy.11.refs_0_, bf16[7,729,128]{2,1,0:T(8,128)(2,1)S(1)} %bitcast.9, bf16[2,729,128]{2,1,0:T(8,128)(2,1)S(1)} %collective-permute-done.refs_2_, s32[1,128]{1,0:T(1,128)S(1)} %copy-done.1, bf16[2,768,128]{2,1,0:T(8,128)(2,1)S(1)} %get-tuple-element.7.refs_4_, ...), custom_call_target="tpu_custom_call" | custom-call | tf_op jit(solution)/shard_map/pallas_call | solution.py:294
  36.1 0.0 all-reduce.2.cloned.1.call-update
  36.1 49.1 %all-reduce.2.cloned.1.call-done = f32[729,256]{1,0:T(8,128)} async-done(((f32[729,256]{1,0:T(8,128)}), f32[729,256]{1,0:T(8,128)}) %all-reduce.2.cloned.1.call-update) | async-done | bytes 746512 | tf_op jit(solution)/shard_map/psum | solution.py:311
  85.1 2.0 %copy.12 = f32[729,256]{1,0:T(8,128)} copy(f32[729,256]{1,0:T(8,128)} %all-reduce.2.cloned.1.call-done) | data formatting | bytes 1492992
Async XLA Ops:
  6.5 78.6 %all-reduce.2.cloned.1.call-start = ((), (), s32[]{:S(2)}) async-start(), calls=%async_computation | async-start | bytes 1507328 | tf_op jit(solution)/shard_map/psum | solution.py:311
  8.1 3.0 %copy-start = (bf16[1,7,729,128]{3,2,1,0:T(8,128)(2,1)S(1)}, bf16[1,7,729,128]{3,2,1,0:T(8,128)(2,1)}, u32[]{:S(2)}) copy-start(bf16[1,7,729,128]{3,2,1,0:T(8,128)(2,1)} %param.7) | copy-start | bytes 3919108
  8.1 3.0 %copy-start.1 = (s32[1,128]{1,0:T(1,128)S(1)}, s32[1,128]{1,0:T(1,128)}, u32[]{:S(2)}) copy-start(s32[1,128]{1,0:T(1,128)} %refs_3_.1) | copy-start | bytes 1540
  8.1 8.1 %copy-start.3 = (s32[128]{0:T(128)S(1)}, s32[128]{0:T(128)}, u32[]{:S(2)}) copy-start(s32[128]{0:T(128)} %param.9) | copy-start | bytes 1540
  8.7 7.5 %collective-permute-start.1 = (bf16[2,729,128]{2,1,0:T(8,128)(2,1)S(1)}, bf16[2,729,128]{2,1,0:T(8,128)(2,1)S(1)}, u32[]{:S(2)}, u32[]{:S(2)}) collective-permute-start(bf16[2,729,128]{2,1,0:T(8,128)(2,1)S(1)} %shard_map.65), channel_id=1, source_target_pairs={{0,1},{1,2},{2,3},{3,4},{4,5},{5,6},{6,7},{8,9},{9,10},{10,11},{11... | collective-permute-start | bytes 1119752 | tf_op jit(solution)/shard_map/ppermute | solution.py:17
  11.1 14.7 %copy-start.2 = (s32[256]{0:T(256)S(1)}, s32[256]{0:T(256)}, u32[]{:S(2)}) copy-start(s32[256]{0:T(256)} %param.10) | copy-start | bytes 3076
  11.7 13.9 %collective-permute-start = (bf16[2,729,128]{2,1,0:T(8,128)(2,1)S(1)}, bf16[2,729,128]{2,1,0:T(8,128)(2,1)S(1)}, u32[]{:S(2)}, u32[]{:S(2)}) collective-permute-start(bf16[2,729,128]{2,1,0:T(8,128)(2,1)S(1)} %shard_map.64), channel_id=1, source_target_pairs={{0,1},{1,2},{2,3},{3,4},{4,5},{5,6},{6,7},{8,9},{9,10},{10,11},{11... | collective-permute-start | bytes 1119752 | tf_op jit(solution)/shard_map/ppermute | solution.py:17
  21.0 4.9 %collective-permute-start.2 = (bf16[2,192,128]{2,1,0:T(8,128)(2,1)S(1)}, bf16[2,192,128]{2,1,0:T(8,128)(2,1)S(1)}, u32[]{:S(2)}, u32[]{:S(2)}) collective-permute-start(bf16[2,192,128]{2,1,0:T(8,128)(2,1)S(1)} %get-tuple-element.8), channel_id=1, source_target_pairs={{0,1},{1,2},{2,3},{3,4},{4,5},{5,6},{6,7},{8,9},{9,10},{10,11},{11... | collective-permute-start | bytes 294920 | tf_op jit(solution)/shard_map/ppermute | solution.py:17
Sparse Core Ops, SparseCore 0:
  36.2 48.8 all-reduce.1
where the time goes:
time: 94.3 us; the launch traced here: 94 us
  waiting for transfers between devices  49.3 us (52%)
  Pallas kernels  16 us (17%)
  between operations  14.2 us (15%)
  starting transfers between devices  10.8 us (11%)
  local copies, waits for them, and re-layouts  3.64 us (4%)
    psum x1, waiting for transfers between devices, shards(): return lax.psum(partial_density, 'orb')  49.1 us
    ppermute x3, starting transfers between devices, shifted_2(): lax.ppermute(value, axis, [(source, source + steps) for source in range(f...  10.8 us
    pallas_call x1, Pallas kernels, shards(): pl.pallas_call(lambda *refs: second_kernel(*refs, table=valued), grid=(sl...  10.2 us
    pallas_call x1, Pallas kernels, shards(): pl.pallas_call(lambda *refs: first_kernel(*refs, table=matrix), out_shape...  4.77 us
    unnamed x10, local copies, waits for them, and re-layouts  3.64 us
  transfers between devices with their start and end apart: 4, of which 2 were waited for; matrix products, arithmetic and copies ran while one was open for 0% of the time, Pallas kernels for 6%

commit v1 on v0

--- a/solution.py
+++ b/solution.py
@@ -217,7 +217,8 @@
 
 
 def second_kernel(
-    counts_ref, waves_ref, halo_ref, flags_ref, s_ref, spill_ref, key_ref, out_ref, x_ref, a_ref, b_ref, coef_ref, *, table
+    counts_ref, waves_ref, halo_ref, flags_ref, s_ref, spill_ref, key_ref, code_ref, top_ref,
+    x_ref, a_ref, b_ref, coef_ref, value_ref, *, table
 ):
     boxes = waves_ref.shape[-1]
     column, octant = local_keys(key_ref, boxes)
@@ -241,12 +242,93 @@
                 both = jnp.concatenate([waves_ref[2 * g + h - 1], halo_ref[h]], 1)
                 x_ref[2 * g + h, 0:ROWS, :] = dot(both, pick)
     slot = pl.program_id(0) * 128 + lax.broadcasted_iota(jnp.int32, (8, 128), 1)
-    live = jnp.where(slot < counts_ref[0], 2.0, 0.0).astype(jnp.float32)
+    live = jnp.where(slot < counts_ref[0], 1.0, 0.0).astype(jnp.float32)
+    padded = value_ref.shape[0]
+    value_ref[ROWS - 1 : padded, :] = jnp.zeros((padded - ROWS + 1, 128), jnp.float32)
 
     def store(row, count, value):
-        out_ref[row : row + count, :] = (value * value * live)[:count]
+        value_ref[row : row + count, :] = (value * live)[:count]
 
     transform(x_ref, a_ref, b_ref, coef_ref, store)
+    code, top = encode(value_ref[...])
+    code_ref[0] = code
+    top_ref[0] = jnp.broadcast_to(top, (8, 128))
+
+
+def encode(value):
+    top = jnp.max(jnp.abs(value), axis=0, keepdims=True)
+    scaled = value * (32767.0 / jnp.maximum(top, 1e-30))
+    return (jnp.round(scaled).astype(jnp.int32).astype(jnp.int16), top)
+
+
+def decode_square(code, top):
+    value = code.astype(jnp.int32).astype(jnp.float32) * (top * np.float32(1.0 / 32767.0))
+    return value * value
+
+
+def reduce_kernel(
+    code_ref, top_ref, out_ref, got_code, got_top, mine_code, mine_top, sum_code, sum_top,
+    code_send, code_recv, top_send, top_recv, sum_send, sum_recv, peak_send, peak_recv, *, count
+):
+    tiles, padded = code_ref.shape[:2]
+    chunk = padded // count
+    me = lax.axis_index("orb")
+    barrier = pltpu.get_barrier_semaphore()
+    for d in range(1, count):
+        pl.semaphore_signal(
+            barrier, inc=1, device_id={"orb": lax.rem(me + d, count)}, device_id_type=pl.DeviceIdType.MESH
+        )
+    pl.semaphore_wait(barrier, count - 1)
+
+    def send(source, target, sends, recvs, d, t):
+        copy = pltpu.make_async_remote_copy(
+            src_ref=source,
+            dst_ref=target.at[d - 1, t],
+            send_sem=sends.at[d - 1, t],
+            recv_sem=recvs.at[d - 1, t],
+            device_id={"orb": lax.rem(me + d, count)},
+            device_id_type=pl.DeviceIdType.MESH,
+        )
+        copy.start()
+        return copy
+
+    def rows(owner):
+        return pl.ds(pl.multiple_of(owner * chunk, chunk), chunk)
+
+    first, second = ({}, {})
+    for t in range(tiles):
+        for d in range(1, count):
+            peer = lax.rem(me + d, count)
+            first[d, t] = (
+                send(top_ref.at[t], got_top, top_send, top_recv, d, t),
+                send(code_ref.at[t, rows(peer)], got_code, code_send, code_recv, d, t),
+            )
+    for t in range(tiles):
+        total = decode_square(code_ref[t, rows(me), :], top_ref[t, 0:1, :])
+        for d in range(1, count):
+            for copy in first[d, t]:
+                copy.wait_recv()
+            total = total + decode_square(got_code[d - 1, t], got_top[d - 1, t, 0:1, :])
+        code, top = encode(jnp.sqrt(2.0 * total))
+        mine_code[t] = code
+        mine_top[t] = jnp.broadcast_to(top, (8, 128))
+        out_ref[rows(me), 128 * t : 128 * (t + 1)] = decode_square(code, top)
+        for d in range(1, count):
+            second[d, t] = (
+                send(mine_top.at[t], sum_top, peak_send, peak_recv, d, t),
+                send(mine_code.at[t], sum_code, sum_send, sum_recv, d, t),
+            )
+    for t in range(tiles):
+        for d in range(1, count):
+            for copy in second[d, t]:
+                copy.wait_recv()
+            owner = lax.rem(me + count - d, count)
+            out_ref[rows(owner), 128 * t : 128 * (t + 1)] = decode_square(
+                sum_code[d - 1, t], sum_top[d - 1, t, 0:1, :]
+            )
+    for pair in list(first.values()) + list(second.values()):
+        for copy in pair:
+            copy.wait_send()
 
 
 def transform_scratch():
@@ -291,10 +373,17 @@
     def whole(shape):
         return pl.BlockSpec(shape, lambda step: (0,) * len(shape))
 
-    partial_density = pl.pallas_call(
+    count = lax.axis_size("orb")
+    padded = -(-ROWS // (16 * count)) * 16 * count
+    chunk = padded // count
+    tiles = slots // 128
+    codes, tops = pl.pallas_call(
         lambda *refs: second_kernel(*refs, table=valued),
-        grid=(slots // 128,),
-        out_shape=jax.ShapeDtypeStruct((ROWS, slots), jnp.float32),
+        grid=(tiles,),
+        out_shape=(
+            jax.ShapeDtypeStruct((tiles, padded, 128), jnp.int16),
+            jax.ShapeDtypeStruct((tiles, 8, 128), jnp.float32),
+        ),
         in_specs=[
             pl.BlockSpec(memory_space=pltpu.SMEM),
             whole(wavelets.shape),
@@ -304,11 +393,31 @@
             whole(spill.shape),
             pl.BlockSpec((1, 128), lambda step: (0, step)),
         ],
-        out_specs=pl.BlockSpec((ROWS, 128), lambda step: (0, step)),
-        scratch_shapes=transform_scratch(),
+        out_specs=(
+            pl.BlockSpec((1, padded, 128), lambda step: (step, 0, 0)),
+            pl.BlockSpec((1, 8, 128), lambda step: (step, 0, 0)),
+        ),
+        scratch_shapes=transform_scratch() + [pltpu.VMEM((padded, 128), jnp.float32)],
         compiler_params=params,
     )(counts, wavelets, waves_halo, leaf_flags, scaling, spill, child_key2.reshape(1, slots))
-    return lax.psum(partial_density, "orb")
+    peers = (count - 1, tiles)
+    density = pl.pallas_call(
+        lambda *refs: reduce_kernel(*refs, count=count),
+        out_shape=jax.ShapeDtypeStruct((padded, slots), jnp.float32),
+        in_specs=[vmem] * 2,
+        out_specs=vmem,
+        scratch_shapes=[
+            pltpu.VMEM(peers + (chunk, 128), jnp.int16),
+            pltpu.VMEM(peers + (8, 128), jnp.float32),
+            pltpu.VMEM((tiles, chunk, 128), jnp.int16),
+            pltpu.VMEM((tiles, 8, 128), jnp.float32),
+            pltpu.VMEM(peers + (chunk, 128), jnp.int16),
+            pltpu.VMEM(peers + (8, 128), jnp.float32),
+        ]
+        + [pltpu.SemaphoreType.DMA(peers)] * 8,
+        compiler_params=pltpu.CompilerParams(collective_id=0, has_side_effects=True),
+    )(codes, tops)
+    return density[:ROWS]
 
 
 def solution(mesh):

time: 94.3 us -> 60.8 us (0.64)
  the two profiles are of different devices: /device:TPU:0 before, /device:TPU:4 now
where the time goes in v1:
time: 60.8 us; the launch traced here: 60.5 us
  Pallas kernels  39.3 us (65%)
  waiting for transfers between devices  8.07 us (13%)
  starting transfers between devices  7.35 us (12%)
  local copies, waits for them, and re-layouts  4.98 us (8%)
  between operations  0.78 us (1%)
    pallas_call x1, Pallas kernels, shards(): pl.pallas_call(lambda *refs: reduce_kernel(*refs, count=count), out_shape...  23.9 us
    pallas_call x1, Pallas kernels, shards(): pl.pallas_call(lambda *refs: second_kernel(*refs, table=valued), grid=(ti...  9.64 us
    ppermute x3, waiting for transfers between devices, shifted_2(): lax.ppermute(value, axis, [(source, source + steps) for source in range(f...  8.07 us
    ppermute x3, starting transfers between devices, shifted_2(): lax.ppermute(value, axis, [(source, source + steps) for source in range(f...  7.35 us
    pallas_call x1, Pallas kernels, shards(): pl.pallas_call(lambda *refs: first_kernel(*refs, table=matrix), out_shape...  4.76 us
    unnamed x13, local copies, waits for them, and re-layouts  2.94 us
    slice x1, local copies, waits for them, and re-layouts, shards(): return density[:ROWS]  2.04 us
  transfers between devices with their start and end apart: 3, of which 2 were waited for; matrix products, arithmetic and copies ran while one was open for 0% of the time, Pallas kernels for 9%

profile of v1, /device:TPU:4, one launch (start us, length us, event | category | flops | bytes accessed | tf_op | source)
XLA Modules:
  0.0 60.5 jit_solution(9807933603985900080)
XLA Ops:
  0.0 1.6 %copy.9 = bf16[1,8,729,128]{3,2,1,0:T(8,128)(2,1)S(1)} copy(bf16[1,8,729,128]{3,1,2,0:T(8,128)(2,1)} %param.6) | data formatting | bytes 2985984 | tf_op args[0]
  1.6 0.0 copy-start
  1.6 0.0 copy-start.3
  1.6 0.0 copy-start.5
  1.6 0.5 shard_map.65
  2.2 1.9 %collective-permute-start.1 = (bf16[2,729,128]{2,1,0:T(8,128)(2,1)S(1)}, bf16[2,729,128]{2,1,0:T(8,128)(2,1)S(1)}, u32[]{:S(2)}, u32[]{:S(2)}) collective-permute-start(bf16[2,729,128]{2,1,0:T(8,128)(2,1)S(1)} %shard_map.65), channel_id=1, source_target_pairs={{0,1},{1,2},{2,3},{3,4},{4,5},{5,6},{6,7},{8,9},{9,10},{10,11},{11... | collective-permute-start | bytes 1119752 | tf_op jit(solution)/shard_map/ppermute | solution.py:17
  4.1 0.0 copy-done
  4.1 0.0 copy-done.3
  4.1 0.0 copy-start.4
  4.1 0.5 shard_map.64
  4.6 3.5 %collective-permute-start = (bf16[2,729,128]{2,1,0:T(8,128)(2,1)S(1)}, bf16[2,729,128]{2,1,0:T(8,128)(2,1)S(1)}, u32[]{:S(2)}, u32[]{:S(2)}) collective-permute-start(bf16[2,729,128]{2,1,0:T(8,128)(2,1)S(1)} %shard_map.64), channel_id=1, source_target_pairs={{0,1},{1,2},{2,3},{3,4},{4,5},{5,6},{6,7},{8,9},{9,10},{10,11},{11... | collective-permute-start | bytes 1119752 | tf_op jit(solution)/shard_map/ppermute | solution.py:17
  8.1 3.8 %collective-permute-done.1.refs_1_ = bf16[2,729,128]{2,1,0:T(8,128)(2,1)S(1)} collective-permute-done((bf16[2,729,128]{2,1,0:T(8,128)(2,1)S(1)}, bf16[2,729,128]{2,1,0:T(8,128)(2,1)S(1)}, u32[]{:S(2)}, u32[]{:S(2)}) %collective-permute-start.1) | collective-permute-done | bytes 373280 | tf_op jit(solution)/shard_map/ppermute | solution.py:17
  12.0 0.0 copy-done.5
  12.0 4.8 %shard_map.66 = (bf16[2,768,128]{2,1,0:T(8,128)(2,1)S(1)}, bf16[2,192,128]{2,1,0:T(8,128)(2,1)S(1)}) custom-call(bf16[8,729,128]{2,1,0:T(8,128)(2,1)S(1)} %bitcast.7, bf16[2,729,128]{2,1,0:T(8,128)(2,1)S(1)} %collective-permute-done.1.refs_1_, s32[1,128]{1,0:T(1,128)S(1)} %bitcast.11), custom_call_target="tpu_custom_call" | custom-call | tf_op jit(solution)/shard_map/pallas_call | solution.py:360
  16.7 1.9 %collective-permute-start.2 = (bf16[2,192,128]{2,1,0:T(8,128)(2,1)S(1)}, bf16[2,192,128]{2,1,0:T(8,128)(2,1)S(1)}, u32[]{:S(2)}, u32[]{:S(2)}) collective-permute-start(bf16[2,192,128]{2,1,0:T(8,128)(2,1)S(1)} %get-tuple-element.10), channel_id=1, source_target_pairs={{0,1},{1,2},{2,3},{3,4},{4,5},{5,6},{6,7},{8,9},{9,10},{10,11},{11... | collective-permute-start | bytes 294920 | tf_op jit(solution)/shard_map/ppermute | solution.py:17
  19.3 0.0 collective-permute-done.refs_2_
  19.3 4.2 %collective-permute-done.2.refs_5_ = bf16[2,192,128]{2,1,0:T(8,128)(2,1)S(1)} collective-permute-done((bf16[2,192,128]{2,1,0:T(8,128)(2,1)S(1)}, bf16[2,192,128]{2,1,0:T(8,128)(2,1)S(1)}, u32[]{:S(2)}, u32[]{:S(2)}) %collective-permute-start.2) | collective-permute-done | bytes 98336 | tf_op jit(solution)/shard_map/ppermute | solution.py:17
  23.6 0.0 copy-done.4
  23.6 9.6 %shard_map.67 = (s16[2,768,128]{2,1,0:T(8,128)(2,1)S(1)}, f32[2,8,128]{2,1,0:T(8,128)S(1)}) custom-call(s32[1]{0:T(128)S(6)} %copy.10.refs_0_, bf16[7,729,128]{2,1,0:T(8,128)(2,1)S(1)} %bitcast.9, bf16[2,729,128]{2,1,0:T(8,128)(2,1)S(1)} %collective-permute-done.refs_2_, s32[1,128]{1,0:T(1,128)S(1)} %copy-done.3, ...), custom_call_target="tpu_custom_call" | custom-call | tf_op jit(solution)/shard_map/pallas_call | solution.py:380
  33.2 0.0 copy-start.1
  33.2 0.7 %copy-done.1 = s16[2,768,128]{2,1,0:T(8,128)(2,1)} copy-done((s16[2,768,128]{2,1,0:T(8,128)(2,1)}, s16[2,768,128]{2,1,0:T(8,128)(2,1)S(1)}, u32[]{:S(2)}) %copy-start.1) | copy-done | bytes 393240
  34.0 0.0 copy-start.2
  34.0 0.6 copy-done.2
  34.6 23.9 %shard_map.68 = f32[768,256]{1,0:T(8,128)} custom-call(s16[2,768,128]{2,1,0:T(8,128)(2,1)} %copy-done.1, f32[2,8,128]{2,1,0:T(8,128)} %copy-done.2), custom_call_target="tpu_custom_call" | custom-call | tf_op jit(solution)/shard_map/pallas_call | solution.py:404
  58.5 2.0 %slice.3 = f32[729,256]{1,0:T(8,128)} slice(f32[768,256]{1,0:T(8,128)} %shard_map.68), slice={[0:729], [0:256]} | slice | bytes 1492992 | tf_op jit(solution)/shard_map/slice | solution.py:420
Async XLA Ops:
  1.6 2.5 %copy-start = (bf16[1,7,729,128]{3,2,1,0:T(8,128)(2,1)S(1)}, bf16[1,7,729,128]{3,2,1,0:T(8,128)(2,1)}, u32[]{:S(2)}) copy-start(bf16[1,7,729,128]{3,2,1,0:T(8,128)(2,1)} %param.7) | copy-start | bytes 3919108
  1.6 2.5 %copy-start.3 = (s32[1,128]{1,0:T(1,128)S(1)}, s32[1,128]{1,0:T(1,128)}, u32[]{:S(2)}) copy-start(s32[1,128]{1,0:T(1,128)} %refs_3_.1) | copy-start | bytes 1540
  1.6 10.4 %copy-start.5 = (s32[128]{0:T(128)S(1)}, s32[128]{0:T(128)}, u32[]{:S(2)}) copy-start(s32[128]{0:T(128)} %param.9) | copy-start | bytes 1540
  2.2 9.8 %collective-permute-start.1 = (bf16[2,729,128]{2,1,0:T(8,128)(2,1)S(1)}, bf16[2,729,128]{2,1,0:T(8,128)(2,1)S(1)}, u32[]{:S(2)}, u32[]{:S(2)}) collective-permute-start(bf16[2,729,128]{2,1,0:T(8,128)(2,1)S(1)} %shard_map.65), channel_id=1, source_target_pairs={{0,1},{1,2},{2,3},{3,4},{4,5},{5,6},{6,7},{8,9},{9,10},{10,11},{11... | collective-permute-start | bytes 1119752 | tf_op jit(solution)/shard_map/ppermute | solution.py:17
  4.1 19.5 %copy-start.4 = (s32[256]{0:T(256)S(1)}, s32[256]{0:T(256)}, u32[]{:S(2)}) copy-start(s32[256]{0:T(256)} %param.10) | copy-start | bytes 3076
  4.6 14.7 %collective-permute-start = (bf16[2,729,128]{2,1,0:T(8,128)(2,1)S(1)}, bf16[2,729,128]{2,1,0:T(8,128)(2,1)S(1)}, u32[]{:S(2)}, u32[]{:S(2)}) collective-permute-start(bf16[2,729,128]{2,1,0:T(8,128)(2,1)S(1)} %shard_map.64), channel_id=1, source_target_pairs={{0,1},{1,2},{2,3},{3,4},{4,5},{5,6},{6,7},{8,9},{9,10},{10,11},{11... | collective-permute-start | bytes 1119752 | tf_op jit(solution)/shard_map/ppermute | solution.py:17
  16.7 6.8 %collective-permute-start.2 = (bf16[2,192,128]{2,1,0:T(8,128)(2,1)S(1)}, bf16[2,192,128]{2,1,0:T(8,128)(2,1)S(1)}, u32[]{:S(2)}, u32[]{:S(2)}) collective-permute-start(bf16[2,192,128]{2,1,0:T(8,128)(2,1)S(1)} %get-tuple-element.10), channel_id=1, source_target_pairs={{0,1},{1,2},{2,3},{3,4},{4,5},{5,6},{6,7},{8,9},{9,10},{10,11},{11... | collective-permute-start | bytes 294920 | tf_op jit(solution)/shard_map/ppermute | solution.py:17
  33.2 0.7 %copy-start.1 = (s16[2,768,128]{2,1,0:T(8,128)(2,1)}, s16[2,768,128]{2,1,0:T(8,128)(2,1)S(1)}, u32[]{:S(2)}) copy-start(s16[2,768,128]{2,1,0:T(8,128)(2,1)S(1)} %get-tuple-element.11.refs_0_) | copy-start | bytes 1179652
  34.0 0.6 copy-start.2
